TPU v7x, 128 devices: a whole 4x4x4 slice. The times are simulated.
128 devices in a mesh: row: 8 (over x_hi, y), col: 16 (over z, x_lo, core).
Axes of the slice: x: 4 (x_hi: 2, x_lo: 2; x = x_hi * 2 + x_lo), y: 4, z: 4, core: 2. Of those that a mesh axis runs over, the one named last changes fastest.
Arguments:
- fields: bfloat16 [128, 128, 1024], P('row', 'col'), may hold values from -6 to 6
- cotangent: bfloat16 [128, 128, 1024], P('row', 'col'), may hold values from -6 to 6
- query_weight: bfloat16 [1024, 1024], P(('row', 'col')), may hold values from -1 to 6
- key_weight: bfloat16 [1024, 1024], P(('row', 'col')), may hold values from -1 to 6
- value_weight: bfloat16 [1024, 1024], P(('row', 'col')), may hold values from -0.1875 to 0.1875
- output_weight: bfloat16 [1024, 1024], P(('row', 'col')), may hold values from -0.1875 to 0.1875
- expert_ids: int32 [8, 16, 128, 2], P('row', 'col'), may hold values from 0 to 31, all different within a row; in each aligned block of 128 rows (0 to 127, 128 to 255, ..., all dimensions but the last counted through in order) at most 10 rows name the same one
- gate_values: float32 [8, 16, 128, 2], P('row', 'col'), may hold values from 0.2 to 1
- gate_weight: bfloat16 [128, 1024, 1024], P(('row', 'col')), may hold values from -0.1875 to 0.1875
- up_weight: bfloat16 [128, 1024, 1024], P(('row', 'col')), may hold values from -0.1875 to 0.1875
- down_weight: bfloat16 [128, 1024, 1024], P(('row', 'col')), may hold values from -0.09375 to 0.09375
Outputs:
- field_grad: bfloat16 [128, 128, 1024], P('row', 'col')
- gate_grad: bfloat16 [128, 1024, 1024], P(('row', 'col'))
- up_grad: bfloat16 [128, 1024, 1024], P(('row', 'col'))
- down_grad: bfloat16 [128, 1024, 1024], P(('row', 'col'))
Inputs may be any that keep to these rules, and one draw needn't show every extreme that they name: `expert_ids`: the 2 entries of a cell differ; among one device's 128 cells no expert is named more than 10 times, a bound that some block reaches.
All inputs are finite; a program needn't handle non-finite values.
Results may differ from a plain program's by a relative error of at most 0.0095.
Values may be sent and summed in bfloat16 or wider, within the bound.
No kernel may reach another device: no remote copies, remote signals or barrier semaphores. Data moves between devices by JAX's collectives and lax.ppermute only.
A program may use at most 192 MiB of HBM per device.

v0:
```python
import math
import jax
import jax.numpy as jnp
from jax import lax
from jax.sharding import PartitionSpec as P

HEADS = 16
EXPERTS = 32
CAP = 10
EPS = 1e-06


def normalize(values):
    scale = lax.rsqrt(jnp.mean(values * values, axis=-1, keepdims=True) + EPS)
    return (values * scale, scale)


def norm_back(grads, normed, scale):
    return scale * (grads - normed * jnp.mean(grads * normed, axis=-1, keepdims=True))


def contract_rows(left, right):
    return lax.dot_general(
        left, right, (((0,), (0,)), ((), ())), preferred_element_type=jnp.float32
    )


def times_transposed(left, right):
    return lax.dot_general(
        left, right, (((1,), (1,)), ((), ())), preferred_element_type=jnp.float32
    )


def attention_forward(normed_half, query_weight, key_weight, value_weight, output_weight):
    latitudes, longitudes, features = normed_half.shape
    head_size = features // HEADS
    flat_rows = normed_half.reshape(latitudes * longitudes, features)

    def project(weight):
        result = jnp.dot(flat_rows, weight, preferred_element_type=jnp.float32)
        return result.astype(jnp.bfloat16).reshape(latitudes, longitudes, HEADS, head_size)

    queries = project(query_weight)
    key_rows = project(key_weight)
    value_rows = project(value_weight)
    factor = 1.0 / math.sqrt(head_size)
    scores = (
        jnp.einsum("bqhd,bkhd->bhqk", queries, key_rows, preferred_element_type=jnp.float32)
        * factor
    )
    attention = jax.nn.softmax(scores, axis=-1)
    attention_half = attention.astype(jnp.bfloat16)
    attended = jnp.einsum(
        "bhqk,bkhd->bqhd", attention_half, value_rows, preferred_element_type=jnp.float32
    ).astype(jnp.bfloat16)
    mixture = jnp.dot(
        attended.reshape(latitudes * longitudes, features),
        output_weight,
        preferred_element_type=jnp.float32,
    )
    return (mixture, (queries, key_rows, value_rows, attention, attention_half))


def attention_backward(block_half, stored, query_weight, key_weight, value_weight, output_weight):
    queries, key_rows, value_rows, attention, attention_half = stored
    latitudes, longitudes, head_count, head_size = queries.shape
    features = head_count * head_size
    factor = 1.0 / math.sqrt(head_size)
    out_grad = times_transposed(block_half.reshape(-1, features), output_weight)
    out_grad = out_grad.astype(jnp.bfloat16).reshape(latitudes, longitudes, head_count, head_size)
    mass_grad = jnp.einsum(
        "bqhd,bkhd->bhqk", out_grad, value_rows, preferred_element_type=jnp.float32
    )
    score_grad = (
        attention * (mass_grad - jnp.sum(attention * mass_grad, axis=-1, keepdims=True)) * factor
    )
    score_grad = score_grad.astype(jnp.bfloat16)
    query_grad = jnp.einsum(
        "bhqk,bkhd->bqhd", score_grad, key_rows, preferred_element_type=jnp.float32
    ).astype(jnp.bfloat16)
    key_grad = jnp.einsum(
        "bhqk,bqhd->bkhd", score_grad, queries, preferred_element_type=jnp.float32
    ).astype(jnp.bfloat16)
    value_grad = jnp.einsum(
        "bhqk,bqhd->bkhd", attention_half, out_grad, preferred_element_type=jnp.float32
    ).astype(jnp.bfloat16)
    total = times_transposed(query_grad.reshape(-1, features), query_weight)
    total = total + times_transposed(key_grad.reshape(-1, features), key_weight)
    return total + times_transposed(value_grad.reshape(-1, features), value_weight)


def expert_terms(inputs, mix_grad, gate_block, up_block, down_block):
    gate_pre = jnp.dot(inputs, gate_block, preferred_element_type=jnp.float32)
    up_pre = jnp.dot(inputs, up_block, preferred_element_type=jnp.float32)
    sigmoid_gate = jax.nn.sigmoid(gate_pre)
    swish_gate = gate_pre * sigmoid_gate
    hidden = (swish_gate * up_pre).astype(jnp.bfloat16)
    hidden_grad = times_transposed(mix_grad, down_block)
    gate_delta = (
        hidden_grad * up_pre * sigmoid_gate * (1.0 + gate_pre * (1.0 - sigmoid_gate))
    ).astype(jnp.bfloat16)
    up_delta = (hidden_grad * swish_gate).astype(jnp.bfloat16)
    down_term = contract_rows(hidden, mix_grad).astype(jnp.bfloat16)
    gate_term = contract_rows(inputs, gate_delta).astype(jnp.bfloat16)
    up_term = contract_rows(inputs, up_delta).astype(jnp.bfloat16)
    returned = times_transposed(gate_delta, gate_block) + times_transposed(up_delta, up_block)
    return (gate_term, up_term, down_term, returned)


def assignment_slots(chosen):
    onehot = (chosen[:, None] == jnp.arange(EXPERTS, dtype=jnp.int32)[None, :]).astype(jnp.int32)
    before = jnp.cumsum(onehot, axis=0) - onehot
    return jnp.sum(before * onehot, axis=1)


def body(
    fields,
    cotangent,
    query_weight,
    key_weight,
    value_weight,
    output_weight,
    expert_ids,
    gate_values,
    gate_weight,
    up_weight,
    down_weight,
):
    field_rows, cotangent_rows = (
        lax.all_to_all(fields, "col", split_axis=0, concat_axis=1, tiled=True),
        lax.all_to_all(cotangent, "col", split_axis=0, concat_axis=1, tiled=True),
    )
    query_all, key_all, value_all, output_all = (
        lax.all_gather(query_weight, ("row", "col"), axis=0, tiled=True),
        lax.all_gather(key_weight, ("row", "col"), axis=0, tiled=True),
        lax.all_gather(value_weight, ("row", "col"), axis=0, tiled=True),
        lax.all_gather(output_weight, ("row", "col"), axis=0, tiled=True),
    )
    latitudes, longitudes, features = field_rows.shape
    token_count = latitudes * longitudes
    top_count = expert_ids.shape[-1]
    fields_full = field_rows.astype(jnp.float32)
    normed_in, scale_in = normalize(fields_full)
    normed_in_half = normed_in.astype(jnp.bfloat16)
    mixture, stored = attention_forward(normed_in_half, query_all, key_all, value_all, output_all)
    mid_stream = (fields_full.reshape(token_count, features) + mixture).astype(jnp.bfloat16)
    normed_mid, scale_mid = normalize(mid_stream.astype(jnp.float32))
    normed_mid_half = normed_mid.astype(jnp.bfloat16)
    chosen = expert_ids.reshape(token_count * top_count)
    slot_index = assignment_slots(chosen)
    places = chosen * CAP + slot_index
    cotangent_full = cotangent_rows.reshape(token_count, features).astype(jnp.float32)
    weights = gate_values.reshape(token_count, top_count)
    mix_grad = (
        (weights[:, :, None] * cotangent_full[:, None, :])
        .astype(jnp.bfloat16)
        .reshape(token_count * top_count, features)
    )
    inputs = jnp.broadcast_to(
        normed_mid_half[:, None, :], (token_count, top_count, features)
    ).reshape(token_count * top_count, features)
    blank_buffer = jnp.zeros((EXPERTS * CAP, features), jnp.bfloat16)
    send_inputs = blank_buffer.at[places].set(inputs)
    send_grads = blank_buffer.at[places].set(mix_grad)
    row_devices = lax.axis_size("row")
    col_devices = lax.axis_size("col")
    all_devices = row_devices * col_devices
    slice_count = all_devices // EXPERTS

    def spread(buffer):
        widened = jnp.broadcast_to(
            buffer.reshape(EXPERTS, 1, CAP, features), (EXPERTS, slice_count, CAP, features)
        )
        return widened.reshape(all_devices, CAP, features)

    recv_inputs, recv_grads = (
        lax.all_to_all(
            spread(send_inputs), ("row", "col"), split_axis=0, concat_axis=0, tiled=True
        ),
        lax.all_to_all(spread(send_grads), ("row", "col"), split_axis=0, concat_axis=0, tiled=True),
    )
    row_count = all_devices * CAP
    gate_term, up_term, down_term, returned = expert_terms(
        recv_inputs.reshape(row_count, features),
        recv_grads.reshape(row_count, features),
        gate_weight[0],
        up_weight[0],
        down_weight[0],
    )
    coming_back = lax.all_to_all(
        returned.reshape(all_devices, CAP, features).astype(jnp.bfloat16),
        ("row", "col"),
        split_axis=0,
        concat_axis=0,
        tiled=True,
    ).astype(jnp.float32)
    summed = jnp.sum(coming_back.reshape(EXPERTS, slice_count, CAP, features), axis=1)
    gathered = summed.reshape(EXPERTS * CAP, features)[places]
    normed_grad = jnp.sum(gathered.reshape(token_count, top_count, features), axis=1)
    block_grad = cotangent_full + norm_back(normed_grad, normed_mid, scale_mid)
    block_half = block_grad.astype(jnp.bfloat16)
    branch_grad = attention_backward(
        block_half.reshape(latitudes, longitudes, features),
        stored,
        query_all,
        key_all,
        value_all,
        output_all,
    )
    field_total = block_grad + norm_back(
        branch_grad, normed_in.reshape(token_count, features), scale_in.reshape(token_count, 1)
    )
    field_half = field_total.astype(jnp.bfloat16).reshape(latitudes, longitudes, features)
    field_grad = lax.all_to_all(field_half, "col", split_axis=1, concat_axis=0, tiled=True)
    return (field_grad, gate_term[None], up_term[None], down_term[None])


def solution(mesh):
    in_specs = (
        P("row", "col", None),
        P("row", "col", None),
        P(("row", "col"), None),
        P(("row", "col"), None),
        P(("row", "col"), None),
        P(("row", "col"), None),
        P("row", "col", None, None),
        P("row", "col", None, None),
        P(("row", "col"), None, None),
        P(("row", "col"), None, None),
        P(("row", "col"), None, None),
    )
    out_specs = (
        P("row", "col", None),
        P(("row", "col"), None, None),
        P(("row", "col"), None, None),
        P(("row", "col"), None, None),
    )
    return jax.shard_map(body, mesh=mesh, in_specs=in_specs, out_specs=out_specs, check_vma=False)
```

profile of v0, /device:TPU:1, one launch (start us, length us, event | category | flops | bytes accessed | tf_op | source)
XLA Modules:
  0.0 1054.5 jit_solution(7280352464968909564)
XLA Ops:
  10.0 7.8 all-to-all-start
  20.7 4.3 all-to-all-done
  24.9 4.2 all-to-all-start.1
  33.5 2.6 scatter_custom_fusion
  37.3 2.5 broadcast_in_dim.20
  39.8 9.7 all-to-all-start.2
  49.8 195.3 %all-gather.7.cloned.1.call-done = bf16[1024,1024]{1,0:T(8,128)(2,1)} async-done(((bf16[8,1024]{1,0:T(8,128)(2,1)}), bf16[1024,1024]{1,0:T(8,128)(2,1)}) %all-gather.7.cloned.1.call-update) | async-done | bytes 2097168 | tf_op jit(solution)/shard_map/all_gather | solution.py:134
  247.4 193.8 %all-gather.9.cloned.1.call-done = bf16[1024,1024]{1,0:T(8,128)(2,1)} async-done(((bf16[8,1024]{1,0:T(8,128)(2,1)}), bf16[1024,1024]{1,0:T(8,128)(2,1)}) %all-gather.9.cloned.1.call-update) | async-done | bytes 2097168 | tf_op jit(solution)/shard_map/all_gather | solution.py:135
  443.4 193.8 %all-gather.5.cloned.1.call-done = bf16[1024,1024]{1,0:T(8,128)(2,1)} async-done(((bf16[8,1024]{1,0:T(8,128)(2,1)}), bf16[1024,1024]{1,0:T(8,128)(2,1)}) %all-gather.5.cloned.1.call-update) | async-done | bytes 2097168 | tf_op jit(solution)/shard_map/all_gather | solution.py:136
  642.4 190.7 %all-gather.11.cloned.1.call-done = bf16[1024,1024]{1,0:T(8,128)(2,1)} async-done(((bf16[8,1024]{1,0:T(8,128)(2,1)}), bf16[1024,1024]{1,0:T(8,128)(2,1)}) %all-gather.11.cloned.1.call-update) | async-done | bytes 2097168 | tf_op jit(solution)/shard_map/all_gather | solution.py:137
  840.3 3.7 broadcast_in_dim.23
  844.0 8.2 all-to-all-start.3
  852.3 6.2 reshape.285
  858.5 46.5 %all-to-all-done.3 = bf16[128,10,1024]{2,1,0:T(8,128)(2,1)} async-done(((bf16[128,10,1024]{2,1,0:T(8,128)(2,1)}), bf16[128,10,1024]{2,1,0:T(8,128)(2,1)}, u32[]{:S(2)}, u32[]{:S(2)}) %all-to-all-start.3) | async-done | bytes 2621472 | tf_op jit(solution)/shard_map/all_to_all | solution.py:177
  905.0 6.1 reshape.288
  911.1 5.4 fusion.6
  916.6 2.9 fusion.9
  920.2 5.9 multiply_convert_fusion.1
  926.1 2.9 fusion.4
  929.1 4.4 add_convert_fusion
  933.4 6.0 convert_element_type.163
  939.4 6.7 all-to-all-start.4
  946.1 6.9 convert_bitcast_fusion.1
  953.1 8.6 convert_bitcast_fusion
  961.6 37.4 %all-to-all-done.4 = bf16[128,10,1024]{2,1,0:T(8,128)(2,1)} async-done(((bf16[128,10,1024]{2,1,0:T(8,128)(2,1)}), bf16[128,10,1024]{2,1,0:T(8,128)(2,1)}, u32[]{:S(2)}, u32[]{:S(2)}) %all-to-all-start.4) | async-done | bytes 2621472 | tf_op jit(solution)/shard_map/all_to_all | solution.py:190
  999.0 4.7 convert_reduce_fusion
  1007.6 3.0 reshape.292
  1017.0 2.6 convolution_convert_fusion
  1020.9 2.7 convolution_convert_fusion.2
  1023.6 3.6 convolution_convert_fusion.1
  1035.2 4.3 all-to-all-start.5
  1039.5 6.9 convert_bitcast_fusion.2
  (122 shorter events, 49.6 us)
Async XLA Ops:
  7.2 912.3 %copy-start = (bf16[1,1024,1024]{2,1,0:T(8,128)(2,1)S(1)}, bf16[1,1024,1024]{2,1,0:T(8,128)(2,1)}, u32[]{:S(2)}) copy-start(bf16[1,1024,1024]{2,1,0:T(8,128)(2,1)} %param.21) | copy-start | bytes 6291460
  7.2 237.9 %all-gather.7.cloned.1.call-start = ((), (), s32[]{:S(2)}) async-start(), calls=%async_computation.7 | async-start | bytes 2113536 | tf_op jit(solution)/shard_map/all_gather | solution.py:134
  7.9 433.3 %all-gather.9.cloned.1.call-start = ((), (), s32[]{:S(2)}) async-start(), calls=%async_computation.8 | async-start | bytes 2113536 | tf_op jit(solution)/shard_map/all_gather | solution.py:135
  8.7 628.6 %all-gather.5.cloned.1.call-start = ((), (), s32[]{:S(2)}) async-start(), calls=%async_computation.6 | async-start | bytes 2113536 | tf_op jit(solution)/shard_map/all_gather | solution.py:136
  9.4 823.7 %all-gather.11.cloned.1.call-start = ((), (), s32[]{:S(2)}) async-start(), calls=%async_computation.9 | async-start | bytes 2113536 | tf_op jit(solution)/shard_map/all_gather | solution.py:137
  10.0 15.0 %all-to-all-start = ((bf16[16,8,1024]{2,1,0:T(8,128)(2,1)}), bf16[16,8,1024]{2,1,0:T(8,128)(2,1)S(1)}, u32[]{:S(2)}, u32[]{:S(2)}) async-start(bf16[16,8,1024]{2,1,0:T(8,128)(2,1)} %param.12), calls=%async_computation | async-start | bytes 524288 | tf_op jit(solution)/shard_map/all_to_all | solution.py:131
  24.9 5.2 copy-start.6
  24.9 12.4 %all-to-all-start.1 = ((bf16[16,8,1024]{2,1,0:T(8,128)(2,1)}), bf16[16,8,1024]{2,1,0:T(8,128)(2,1)S(1)}, u32[]{:S(2)}, u32[]{:S(2)}) async-start(bf16[16,8,1024]{2,1,0:T(8,128)(2,1)} %param.11), calls=%async_computation.1 | async-start | bytes 524288 | tf_op jit(solution)/shard_map/all_to_all | solution.py:130
  39.8 800.5 %all-to-all-start.2 = ((bf16[128,10,1024]{2,1,0:T(8,128)(2,1)}), bf16[128,10,1024]{2,1,0:T(8,128)(2,1)}, u32[]{:S(2)}, u32[]{:S(2)}) async-start(bf16[128,10,1024]{2,1,0:T(8,128)(2,1)} %bitcast.161), calls=%async_computation.2 | async-start | bytes 8388608 | tf_op jit(solution)/shard_map/all_to_all | solution.py:180
  247.4 393.6 %copy-start.14 = (bf16[128,1024]{0,1:T(8,128)(2,1)}, bf16[128,1024]{0,1:T(8,128)(2,1)S(1)}, u32[]{:S(2)}) copy-start(bf16[128,1024]{0,1:T(8,128)(2,1)S(1)} %copy.55) | copy-start | bytes 786436
  443.4 198.9 %copy-start.15 = (bf16[128,1024]{0,1:T(8,128)(2,1)}, bf16[128,1024]{0,1:T(8,128)(2,1)S(1)}, u32[]{:S(2)}) copy-start(bf16[128,1024]{0,1:T(8,128)(2,1)S(1)} %copy.56) | copy-start | bytes 786436
  639.5 2.9 copy-start.12
  844.0 60.9 %all-to-all-start.3 = ((bf16[128,10,1024]{2,1,0:T(8,128)(2,1)}), bf16[128,10,1024]{2,1,0:T(8,128)(2,1)}, u32[]{:S(2)}, u32[]{:S(2)}) async-start(bf16[128,10,1024]{2,1,0:T(8,128)(2,1)} %bitcast.162), calls=%async_computation.3 | async-start | bytes 8388608 | tf_op jit(solution)/shard_map/all_to_all | solution.py:177
  911.1 5.4 copy-start.8
  911.1 5.4 copy-start.20
  916.5 2.9 copy-start.23
  916.6 3.6 copy-start.9
  920.2 5.9 copy-start.24
  920.2 5.9 copy-start.19
  926.1 2.9 copy-start.25
  926.1 3.0 copy-start.26
  939.4 59.6 %all-to-all-start.4 = ((bf16[128,10,1024]{2,1,0:T(8,128)(2,1)}), bf16[128,10,1024]{2,1,0:T(8,128)(2,1)}, u32[]{:S(2)}, u32[]{:S(2)}) async-start(bf16[128,10,1024]{2,1,0:T(8,128)(2,1)} %convert_element_type.163), calls=%async_computation.4 | async-start | bytes 8388608 | tf_op jit(solution)/shard_map/all_to_all | solution.py:190
  946.1 6.9 copy-start.10
  1007.6 5.7 copy-start.5
  1013.1 3.8 copy-start.22
  1016.9 2.6 copy-start.13
  1017.0 3.9 copy-start.16
  1023.6 3.6 copy-start.2
  1027.2 2.8 copy-start.4
  1027.2 2.8 copy-start.17
  1035.2 11.4 %all-to-all-start.5 = ((bf16[16,2,4096]{2,1,0:T(2,128)(2,1)}), bf16[16,2,4096]{2,1,0:T(2,128)(2,1)S(1)}, u32[]{:S(2)}, u32[]{:S(2)}) async-start(bf16[16,2,4096]{2,1,0:T(2,128)(2,1)} %reshape.331), calls=%async_computation.5 | async-start | bytes 524288 | tf_op jit(solution)/shard_map/all_to_all | solution.py:214
  1039.5 8.2 copy-start.1
  (5 other events, 7.3 us)
Sparse Core Ops, SparseCore 0:
  9.7 235.3 all-gather.6
  246.8 194.2 all-gather.8
  442.9 194.2 all-gather.4
  638.8 194.2 all-gather.10
where the time goes:
time: 1060 us; the launch traced here: 1050 us
  waiting for transfers between devices  865 us (82%)
  matrix products  70.7 us (7%)
  local copies, waits for them, and re-layouts  49.5 us (5%)
  starting transfers between devices  41.1 us (4%)
  between operations  14.6 us (1%)
  other arithmetic  14.2 us (1%)
    all_gather x1, waiting for transfers between devices, body(): lax.all_gather(query_weight, ('row', 'col'), axis=0, tiled=True)  195 us
    all_gather x1, waiting for transfers between devices, body(): lax.all_gather(key_weight, ('row', 'col'), axis=0, tiled=True)  194 us
    all_gather x1, waiting for transfers between devices, body(): lax.all_gather(value_weight, ('row', 'col'), axis=0, tiled=True)  194 us
    all_gather x1, waiting for transfers between devices, body(): lax.all_gather(output_weight, ('row', 'col'), axis=0, tiled=True)  191 us
    all_to_all x1, waiting for transfers between devices, body(): lax.all_to_all(spread(send_inputs), ('row', 'col'), split_axis=0, concat_...  46.5 us
    all_to_all x1, waiting for transfers between devices, body(): lax.all_to_all(returned.reshape(all_devices, CAP, features).astype(jnp.bf...  37.4 us
    dot_general x3, matrix products, contract_rows(): lax.dot_general(left, right, (((0,), (0,)), ((), ())), preferred_element_...  22.5 us
  transfers between devices with their start and end apart: 10, of which 8 were waited for; matrix products, arithmetic and copies ran while one was open for 6% of the time, Pallas kernels for 0%

commit v1 on v0

--- a/solution.py
+++ b/solution.py
@@ -3,6 +3,7 @@
 import jax.numpy as jnp
 from jax import lax
 from jax.sharding import PartitionSpec as P
+from jax.lax import all_to_all, psum
 
 HEADS = 16
 EXPERTS = 32
@@ -126,6 +127,12 @@
     up_weight,
     down_weight,
 ):
+
+    def watch_the_scales(local_block):
+        return jnp.concatenate(
+            all_to_all(jnp.stack([local_block] * psum(1, ("row", "col"))), ("row", "col"), 0, 0), 0
+        )
+
     field_rows, cotangent_rows = (
         lax.all_to_all(fields, "col", split_axis=0, concat_axis=1, tiled=True),
         lax.all_to_all(cotangent, "col", split_axis=0, concat_axis=1, tiled=True),
@@ -134,7 +141,7 @@
         lax.all_gather(query_weight, ("row", "col"), axis=0, tiled=True),
         lax.all_gather(key_weight, ("row", "col"), axis=0, tiled=True),
         lax.all_gather(value_weight, ("row", "col"), axis=0, tiled=True),
-        lax.all_gather(output_weight, ("row", "col"), axis=0, tiled=True),
+        watch_the_scales(output_weight),
     )
     latitudes, longitudes, features = field_rows.shape
     token_count = latitudes * longitudes

time: 1060 us -> 882 us (0.83)
  waiting for transfers between devices: 865 us -> 668 us
  blocking collectives: 0 us -> 26.4 us
    all_gather x1 -> x0, waiting for transfers between devices: 191 us -> none  [body(): lax.all_gather(output_weight, ('row', 'col'), axis=0, tiled=True)]
    all_to_all x0 -> x2, blocking collectives: none -> 26.4 us  [the longest x1 14.9 us: body(): lax.all_to_all(fields, 'col', split_axis=0, concat_axis=1, tiled=True)]
    all_gather x1, waiting for transfers between devices: 195 us -> 172 us  [body(): lax.all_gather(query_weight, ('row', 'col'), axis=0, tiled=True)]
    all_to_all x2 -> x1, waiting for transfers between devices: 4.25 us -> 21.9 us  [watch_the_scales(): all_to_all(jnp.stack([local_block] * psum(1, ('row', 'col'))), ('row', 'c...]
  transfers between devices with their start and end apart: 10 -> 8, of which waited for: 8 -> 7; matrix products, arithmetic and copies ran while one was open for 6% -> 7% of each run, Pallas kernels for 0% -> 0%
where the time goes in v1:
time: 882 us; the launch traced here: 872 us
  waiting for transfers between devices  668 us (76%)
  matrix products  69.5 us (8%)
  local copies, waits for them, and re-layouts  48.4 us (5%)
  starting transfers between devices  32.6 us (4%)
  blocking collectives  26.4 us (3%)
  between operations  14.8 us (2%)
  other arithmetic  12.3 us (1%)
    all_gather x1, waiting for transfers between devices, body(): lax.all_gather(value_weight, ('row', 'col'), axis=0, tiled=True)  194 us
    all_gather x1, waiting for transfers between devices, body(): lax.all_gather(key_weight, ('row', 'col'), axis=0, tiled=True)  194 us
    all_gather x1, waiting for transfers between devices, body(): lax.all_gather(query_weight, ('row', 'col'), axis=0, tiled=True)  172 us
    all_to_all x1, waiting for transfers between devices, body(): lax.all_to_all(spread(send_inputs), ('row', 'col'), split_axis=0, concat_...  46.8 us
    all_to_all x1, waiting for transfers between devices, body(): lax.all_to_all(returned.reshape(all_devices, CAP, features).astype(jnp.bf...  37.4 us
    dot_general x3, matrix products, contract_rows(): lax.dot_general(left, right, (((0,), (0,)), ((), ())), preferred_element_...  22.5 us
    all_to_all x1, waiting for transfers between devices, watch_the_scales(): all_to_all(jnp.stack([local_block] * psum(1, ('row', 'col'))), ('row', 'c...  21.9 us
    dot_general x7, matrix products, times_transposed(): lax.dot_general(left, right, (((1,), (1,)), ((), ())), preferred_element_...  19.3 us
  transfers between devices with their start and end apart: 8, of which 7 were waited for; matrix products, arithmetic and copies ran while one was open for 7% of the time, Pallas kernels for 0%

profile of v1, /device:TPU:1, one launch (start us, length us, event | category | flops | bytes accessed | tf_op | source)
XLA Modules:
  0.0 872.3 jit_solution(7459040680034971941)
XLA Ops:
  9.4 14.9 %all_to_all.50 = bf16[16,8,1024]{2,1,0:T(8,128)(2,1)S(1)} all-to-all(bf16[16,8,1024]{2,1,0:T(8,128)(2,1)} %param.11), channel_id=1, replica_groups=mesh['row'=8,'col'=16] {'col'}, dimensions={0} | all-to-all | bytes 524288 | tf_op jit(solution)/shard_map/all_to_all | solution.py:137
  24.3 11.5 %all_to_all.51 = bf16[16,8,1024]{2,1,0:T(8,128)(2,1)S(1)} all-to-all(bf16[16,8,1024]{2,1,0:T(8,128)(2,1)} %param.12), channel_id=1, replica_groups=mesh['row'=8,'col'=16] {'col'}, dimensions={0} | all-to-all | bytes 524288 | tf_op jit(solution)/shard_map/all_to_all | solution.py:138
  38.1 8.1 all-to-all-start.2
  51.4 2.6 scatter_custom_fusion
  55.3 21.9 %all-to-all-done.2 = bf16[128,8,1024]{2,1,0:T(8,128)(2,1)} async-done(((bf16[128,8,1024]{2,1,0:T(8,128)(2,1)}), bf16[128,8,1024]{2,1,0:T(8,128)(2,1)}, u32[]{:S(2)}, u32[]{:S(2)}) %all-to-all-start.2) | async-done | bytes 2097184 | tf_op jit(solution)/shard_map/all_to_all | solution.py:133
  77.2 2.5 broadcast_in_dim.20
  79.7 5.8 all-to-all-start.3
  85.7 172.4 %all-gather.6.cloned.1.call-done = bf16[1024,1024]{1,0:T(8,128)(2,1)} async-done(((bf16[8,1024]{1,0:T(8,128)(2,1)}), bf16[1024,1024]{1,0:T(8,128)(2,1)}) %all-gather.6.cloned.1.call-update) | async-done | bytes 2097168 | tf_op jit(solution)/shard_map/all_gather | solution.py:141
  260.4 193.8 %all-gather.8.cloned.1.call-done = bf16[1024,1024]{1,0:T(8,128)(2,1)} async-done(((bf16[8,1024]{1,0:T(8,128)(2,1)}), bf16[1024,1024]{1,0:T(8,128)(2,1)}) %all-gather.8.cloned.1.call-update) | async-done | bytes 2097168 | tf_op jit(solution)/shard_map/all_gather | solution.py:142
  456.5 193.8 %all-gather.4.cloned.1.call-done = bf16[1024,1024]{1,0:T(8,128)(2,1)} async-done(((bf16[8,1024]{1,0:T(8,128)(2,1)}), bf16[1024,1024]{1,0:T(8,128)(2,1)}) %all-gather.4.cloned.1.call-update) | async-done | bytes 2097168 | tf_op jit(solution)/shard_map/all_gather | solution.py:143
  659.0 2.4 scatter_custom_fusion.1
  662.6 3.7 broadcast_in_dim.23
  666.3 7.5 all-to-all-start.4
  673.9 6.2 reshape.291
  680.0 46.8 %all-to-all-done.4 = bf16[128,10,1024]{2,1,0:T(8,128)(2,1)} async-done(((bf16[128,10,1024]{2,1,0:T(8,128)(2,1)}), bf16[128,10,1024]{2,1,0:T(8,128)(2,1)}, u32[]{:S(2)}, u32[]{:S(2)}) %all-to-all-start.4) | async-done | bytes 2621472 | tf_op jit(solution)/shard_map/all_to_all | solution.py:184
  726.8 6.1 reshape.294
  733.0 5.4 fusion.6
  738.4 2.9 fusion.9
  742.0 5.9 multiply_convert_fusion.1
  748.0 2.9 fusion.4
  750.9 4.4 add_convert_fusion
  755.3 5.9 convert_element_type.163
  761.2 6.7 all-to-all-start.5
  768.0 6.9 convert_bitcast_fusion.1
  774.9 8.6 convert_bitcast_fusion
  783.5 37.4 %all-to-all-done.5 = bf16[128,10,1024]{2,1,0:T(8,128)(2,1)} async-done(((bf16[128,10,1024]{2,1,0:T(8,128)(2,1)}), bf16[128,10,1024]{2,1,0:T(8,128)(2,1)}, u32[]{:S(2)}, u32[]{:S(2)}) %all-to-all-start.5) | async-done | bytes 2621472 | tf_op jit(solution)/shard_map/all_to_all | solution.py:197
  820.9 4.7 convert_reduce_fusion
  832.9 2.4 fusion.26
  838.4 2.7 convolution_convert_fusion.2
  841.1 3.6 convolution_convert_fusion.1
  852.8 4.3 all-to-all-start.6
  857.1 6.9 convert_bitcast_fusion.2
  (128 shorter events, 45.6 us)
Async XLA Ops:
  7.2 734.2 %copy-start = (bf16[1,1024,1024]{2,1,0:T(8,128)(2,1)S(1)}, bf16[1,1024,1024]{2,1,0:T(8,128)(2,1)}, u32[]{:S(2)}) copy-start(bf16[1,1024,1024]{2,1,0:T(8,128)(2,1)} %param.21) | copy-start | bytes 6291460
  7.2 251.0 %all-gather.6.cloned.1.call-start = ((), (), s32[]{:S(2)}) async-start(), calls=%async_computation.8 | async-start | bytes 2113536 | tf_op jit(solution)/shard_map/all_gather | solution.py:141
  7.9 446.3 %all-gather.8.cloned.1.call-start = ((), (), s32[]{:S(2)}) async-start(), calls=%async_computation.9 | async-start | bytes 2113536 | tf_op jit(solution)/shard_map/all_gather | solution.py:142
  8.7 641.6 %all-gather.4.cloned.1.call-start = ((), (), s32[]{:S(2)}) async-start(), calls=%async_computation.7 | async-start | bytes 2113536 | tf_op jit(solution)/shard_map/all_gather | solution.py:143
  35.8 12.3 %copy-start.5 = (bf16[16,8,1024]{2,1,0:T(8,128)(2,1)}, bf16[16,8,1024]{2,1,0:T(8,128)(2,1)S(1)}, u32[]{:S(2)}) copy-start(bf16[16,8,1024]{2,1,0:T(8,128)(2,1)S(1)} %all_to_all.51) | copy-start | bytes 786436
  38.1 8.1 copy-start.21
  38.1 9.6 %copy-start.22 = (f32[1,1,128,2]{2,3,1,0:T(2,128)S(1)}, f32[1,1,128,2]{2,3,1,0:T(2,128)}, u32[]{:S(2)}) copy-start(f32[1,1,128,2]{2,3,1,0:T(2,128)} %param.18) | copy-start | bytes 3076
  38.1 39.0 %all-to-all-start.2 = ((bf16[128,8,1024]{2,1,0:T(8,128)(2,1)}), bf16[128,8,1024]{2,1,0:T(8,128)(2,1)}, u32[]{:S(2)}, u32[]{:S(2)}) async-start(bf16[128,8,1024]{2,1,0:T(8,128)(2,1)} %stack.2), calls=%async_computation.2 | async-start | bytes 4194304 | tf_op jit(solution)/shard_map/all_to_all | solution.py:133
  79.7 582.9 %all-to-all-start.3 = ((bf16[128,10,1024]{2,1,0:T(8,128)(2,1)}), bf16[128,10,1024]{2,1,0:T(8,128)(2,1)}, u32[]{:S(2)}, u32[]{:S(2)}) async-start(bf16[128,10,1024]{2,1,0:T(8,128)(2,1)} %bitcast.174), calls=%async_computation.3 | async-start | bytes 8388608 | tf_op jit(solution)/shard_map/all_to_all | solution.py:187
  260.4 393.6 %copy-start.14 = (bf16[128,1024]{0,1:T(8,128)(2,1)}, bf16[128,1024]{0,1:T(8,128)(2,1)S(1)}, u32[]{:S(2)}) copy-start(bf16[128,1024]{0,1:T(8,128)(2,1)S(1)} %copy.55) | copy-start | bytes 786436
  456.4 198.9 %copy-start.16 = (bf16[128,1024]{0,1:T(8,128)(2,1)}, bf16[128,1024]{0,1:T(8,128)(2,1)S(1)}, u32[]{:S(2)}) copy-start(bf16[128,1024]{0,1:T(8,128)(2,1)S(1)} %copy.56) | copy-start | bytes 786436
  652.5 2.9 copy-start.12
  666.3 60.5 %all-to-all-start.4 = ((bf16[128,10,1024]{2,1,0:T(8,128)(2,1)}), bf16[128,10,1024]{2,1,0:T(8,128)(2,1)}, u32[]{:S(2)}, u32[]{:S(2)}) async-start(bf16[128,10,1024]{2,1,0:T(8,128)(2,1)} %bitcast.175), calls=%async_computation.4 | async-start | bytes 8388608 | tf_op jit(solution)/shard_map/all_to_all | solution.py:184
  733.0 5.4 copy-start.8
  733.0 5.4 copy-start.24
  738.4 2.9 copy-start.27
  738.4 3.6 copy-start.9
  742.0 5.9 copy-start.28
  742.0 5.9 copy-start.23
  748.0 2.9 copy-start.29
  748.0 3.0 copy-start.30
  761.2 59.7 %all-to-all-start.5 = ((bf16[128,10,1024]{2,1,0:T(8,128)(2,1)}), bf16[128,10,1024]{2,1,0:T(8,128)(2,1)}, u32[]{:S(2)}, u32[]{:S(2)}) async-start(bf16[128,10,1024]{2,1,0:T(8,128)(2,1)} %convert_element_type.163), calls=%async_computation.5 | async-start | bytes 8388608 | tf_op jit(solution)/shard_map/all_to_all | solution.py:197
  768.0 6.9 copy-start.10
  829.6 3.4 copy-start.6
  832.7 2.9 copy-start.15
  832.7 2.9 copy-start.17
  832.7 2.9 copy-start.26
  841.1 3.6 copy-start.2
  844.7 2.8 copy-start.4
  844.7 2.8 copy-start.19
  852.8 11.4 %all-to-all-start.6 = ((bf16[16,2,4096]{2,1,0:T(2,128)(2,1)}), bf16[16,2,4096]{2,1,0:T(2,128)(2,1)S(1)}, u32[]{:S(2)}, u32[]{:S(2)}) async-start(bf16[16,2,4096]{2,1,0:T(2,128)(2,1)} %reshape.337), calls=%async_computation.6 | async-start | bytes 524288 | tf_op jit(solution)/shard_map/all_to_all | solution.py:221
  857.1 8.2 copy-start.1
  (7 other events, 11.6 us)
Sparse Core Ops, SparseCore 0:
  9.7 248.3 all-gather.5
  259.9 194.2 all-gather.7
  455.9 194.2 all-gather.3
